TPU v7x, 512 devices: a whole 4x4x16 slice. The times are simulated.
512 devices in a mesh: req: 64 (over z, y), head: 8 (over x, core).
Axes of the slice: x: 4, y: 4, z: 16, core: 2. Of those that a mesh axis runs over, the one named last changes fastest.
Arguments:
- inner_input: bfloat16 [16384, 16384], P('req', 'head'), may hold values from -6 to 6
- projection_input: bfloat16 [16384, 8, 2, 128], P('req', 'head'), may hold values from -6 to 6
- step_before_bias: bfloat16 [16384, 256], P('req', 'head'), may hold values from -2 to 11
- inner_conv_taps: float32 [4, 16384], P(None, 'head'), may hold values from -3 to 3
- projection_conv_taps: float32 [4, 8, 2, 128], P(None, 'head'), may hold values from -3 to 3
- step_bias: float32 [256], P('head'), may hold values from -4.5 to -3.5
- head_decay_rate: float32 [256], P('head'), may hold values from 0.1 to 3
- head_skip_gain: float32 [256], P('head'), may hold values from 0.5 to 1.5
- group_norm_gain: float32 [16384], P('head'), may hold values from 0.5 to 1.5
- tenant: int32 [64], P('req'), may hold values from 0 to 63
- tenant_adapter_row: int32 [64], replicated, may hold values from 0 to 63, each once
- cache_holder_index: int32 [64], P('req'), may hold values from 0 to 63, as said below
- cache_slot_index: int32 [64], P('req'), may hold values from 0 to 1
- adapter_down_panels: bfloat16 [64, 16384, 64], P('req', 'head'), may hold values from -0.046875 to 0.046875
- adapter_up_panels: bfloat16 [64, 64, 8192], P('req', None, 'head'), may hold values from -0.75 to 0.75
- cached_ssm_states: bfloat16 [128, 256, 64, 128], P('req', 'head'), may hold values from -2.5 to 2.5
- inner_conv_cache: bfloat16 [128, 3, 16384], P('req', None, 'head'), may hold values from -6 to 6
- projection_conv_cache: bfloat16 [128, 3, 8, 2, 128], P('req', None, 'head'), may hold values from -6 to 6
Outputs:
- normed_output: bfloat16 [16384, 16384], P('req', 'head')
- adapter_output_term: bfloat16 [16384, 8192], P('req', 'head')
- updated_state: bfloat16 [64, 256, 64, 128], P('req', 'head')
Inputs may be any that keep to these rules, and one draw needn't show every extreme that they name: `tenant_adapter_row`: every row of the adapter tables belongs to exactly one tenant. `cache_holder_index`: no two requests share a cache slot, and each index of req holds the cached states of exactly 1 request.
All inputs are finite; a program needn't handle non-finite values.
Results may differ from a plain program's by a relative error of at most 0.013.
Values may be sent and summed in bfloat16 or wider, within the bound.
No kernel may reach another device: no remote copies, remote signals or barrier semaphores. Data moves between devices by JAX's collectives and lax.ppermute only.
A program may use at most 64 MiB of HBM per device.

v0:
```python
import jax
import jax.numpy as jnp
from jax import lax
from jax.sharding import PartitionSpec as P

ADAPTER_SCALE = 2.0
NORM_EPSILON = 1e-05


def causal_conv(cached, current, weight):
    joined = jnp.concatenate([cached, current], axis=1)
    length_value = current.shape[1]
    summed = weight[0] * joined[:, 0:length_value]
    for tap in range(1, weight.shape[0]):
        summed = summed + weight[tap] * joined[:, tap : tap + length_value]
    return jax.nn.silu(summed).astype(jnp.bfloat16)


def per_device(
    inner_input,
    projection_input,
    step_before_bias,
    inner_conv_taps,
    projection_conv_taps,
    step_bias,
    head_decay_rate,
    head_skip_gain,
    group_norm_gain,
    tenant,
    tenant_adapter_row,
    cache_holder_index,
    cache_slot_index,
    adapter_down_panels,
    adapter_up_panels,
    cached_ssm_states,
    inner_conv_cache,
    projection_conv_cache,
):
    per_device_share = tenant.shape[0]
    slots_dev = cached_ssm_states.shape[0]
    hidden_features_on_card = inner_input.shape[1]
    heads_dev = step_before_bias.shape[1]
    groups_dev = projection_input.shape[1]
    state_size = projection_input.shape[3]
    head_size = hidden_features_on_card // heads_dev
    per_group = heads_dev // groups_dev
    reduced_width = adapter_down_panels.shape[2]
    model_per_device = adapter_up_panels.shape[2]
    tap_count = inner_conv_taps.shape[0]
    length_value = inner_input.shape[0] // per_device_share
    tenant_all, owner_all, slot_all = (
        lax.all_gather(tenant, "req", axis=0, tiled=True),
        lax.all_gather(cache_holder_index, "req", axis=0, tiled=True),
        lax.all_gather(cache_slot_index, "req", axis=0, tiled=True),
    )
    customer_identifiers = jnp.arange(tenant_adapter_row.shape[0], dtype=jnp.int32)
    picked_customer_matrix_pair = jnp.sum(
        jnp.where(
            tenant_all[:, None] == customer_identifiers[None, :], tenant_adapter_row[None, :], 0
        ),
        axis=1,
    )
    ssm_flat = cached_ssm_states.reshape(slots_dev, -1)
    convx_flat = inner_conv_cache.reshape(slots_dev, -1)
    convbc_flat = projection_conv_cache.reshape(slots_dev, -1)
    cache_pick = owner_all * slots_dev + slot_all
    dispersion_factor = (
        lax.all_to_all(
            adapter_down_panels.reshape(adapter_down_panels.shape[0], -1),
            "req",
            split_axis=1,
            concat_axis=0,
            tiled=True,
        ),
        lax.all_to_all(
            adapter_up_panels.reshape(adapter_up_panels.shape[0], -1),
            "req",
            split_axis=1,
            concat_axis=0,
            tiled=True,
        ),
        lax.all_to_all(ssm_flat, "req", split_axis=1, concat_axis=0, tiled=True),
        lax.all_to_all(convx_flat, "req", split_axis=1, concat_axis=0, tiled=True),
        lax.all_to_all(convbc_flat, "req", split_axis=1, concat_axis=0, tiled=True),
    )
    picked_left_factor = jnp.take(dispersion_factor[0], picked_customer_matrix_pair, axis=0)
    picked_right_factor = jnp.take(dispersion_factor[1], picked_customer_matrix_pair, axis=0)
    chosen_state = jnp.take(dispersion_factor[2], cache_pick, axis=0)
    chosen_convx = jnp.take(dispersion_factor[3], cache_pick, axis=0)
    chosen_convbc = jnp.take(dispersion_factor[4], cache_pick, axis=0)
    fetched = (
        lax.all_to_all(picked_left_factor, "req", split_axis=0, concat_axis=1, tiled=True),
        lax.all_to_all(picked_right_factor, "req", split_axis=0, concat_axis=1, tiled=True),
        lax.all_to_all(chosen_state, "req", split_axis=0, concat_axis=1, tiled=True),
        lax.all_to_all(chosen_convx, "req", split_axis=0, concat_axis=1, tiled=True),
        lax.all_to_all(chosen_convbc, "req", split_axis=0, concat_axis=1, tiled=True),
    )
    down_panel = fetched[0].reshape(per_device_share, hidden_features_on_card, reduced_width)
    up_panel = fetched[1].reshape(per_device_share, reduced_width, model_per_device)
    cached_state = fetched[2].reshape(
        per_device_share, groups_dev, per_group, head_size, state_size
    )
    cached_x = fetched[3].reshape(per_device_share, tap_count - 1, hidden_features_on_card)
    cached_bc = fetched[4].reshape(per_device_share, tap_count - 1, groups_dev, 2, state_size)
    conv_x = causal_conv(
        cached_x,
        inner_input.reshape(per_device_share, length_value, hidden_features_on_card),
        inner_conv_taps,
    )
    conv_bc = causal_conv(
        cached_bc,
        projection_input.reshape(per_device_share, length_value, groups_dev, 2, state_size),
        projection_conv_taps,
    )
    b_proj = conv_bc[:, :, :, 0]
    c_proj = conv_bc[:, :, :, 1]
    step_size = jax.nn.softplus(step_before_bias.astype(jnp.float32) + step_bias).reshape(
        per_device_share, length_value, heads_dev
    )
    log_decay = jnp.cumsum(-head_decay_rate * step_size, axis=1)
    log_decay5 = log_decay.reshape(per_device_share, length_value, groups_dev, per_group)
    step_size5 = step_size.reshape(per_device_share, length_value, groups_dev, per_group)
    score_bc = jnp.einsum("rtgn,rsgn->rgts", c_proj, b_proj, preferred_element_type=jnp.float32)
    decay_rows = jnp.transpose(log_decay5, (0, 2, 3, 1))
    log_gap = decay_rows[..., :, None] - decay_rows[..., None, :]
    token_ids = jnp.arange(length_value, dtype=jnp.int32)
    causal = token_ids[:, None] >= token_ids[None, :]
    decay_factor = jnp.exp(jnp.where(causal, log_gap, -jnp.inf))
    step_rows = jnp.transpose(step_size5, (0, 2, 3, 1))
    mix_weights = (score_bc[:, :, None] * decay_factor * step_rows[..., None, :]).astype(
        jnp.bfloat16
    )
    conv_heads = conv_x.reshape(per_device_share, length_value, groups_dev, per_group, head_size)
    intra = jnp.einsum(
        "rghts,rsghp->rtghp", mix_weights, conv_heads, preferred_element_type=jnp.float32
    )
    inter = (
        jnp.einsum("rtgn,rghpn->rtghp", c_proj, cached_state, preferred_element_type=jnp.float32)
        * jnp.exp(log_decay5)[..., None]
    )
    skip_gain = head_skip_gain.reshape(groups_dev, per_group)[..., None]
    mixed = intra + inter + skip_gain * conv_heads
    mean_square = jnp.mean(mixed * mixed, axis=(3, 4), keepdims=True)
    normed_output = (
        (mixed * lax.rsqrt(mean_square + NORM_EPSILON)).reshape(
            per_device_share, length_value, hidden_features_on_card
        )
        * group_norm_gain
    ).astype(jnp.bfloat16)
    low_partial = jnp.einsum(
        "rtc,rcq->rtq", normed_output, down_panel, preferred_element_type=jnp.float32
    )
    reduced_rank = lax.psum(low_partial, "head").astype(jnp.bfloat16)
    adapter_output_term = (
        jnp.einsum("rtq,rqd->rtd", reduced_rank, up_panel, preferred_element_type=jnp.float32)
        * ADAPTER_SCALE
    ).astype(jnp.bfloat16)
    log_total = log_decay[:, -1:, :]
    carry_weight = (jnp.exp(log_total - log_decay) * step_size).reshape(
        per_device_share, length_value, groups_dev, per_group
    )
    carried = (conv_heads * carry_weight[..., None]).astype(jnp.bfloat16)
    fresh_state = jnp.einsum(
        "rsghp,rsgn->rghpn", carried, b_proj, preferred_element_type=jnp.float32
    )
    keep_factor = jnp.exp(log_total[:, 0]).reshape(per_device_share, groups_dev, per_group)[
        ..., None, None
    ]
    updated_state = fresh_state + keep_factor * cached_state
    return (
        normed_output.reshape(per_device_share * length_value, hidden_features_on_card),
        adapter_output_term.reshape(per_device_share * length_value, model_per_device),
        updated_state.reshape(per_device_share, heads_dev, head_size, state_size).astype(
            jnp.bfloat16
        ),
    )


def solution(mesh):
    return jax.shard_map(
        per_device,
        mesh=mesh,
        in_specs=(
            P("req", "head"),
            P("req", "head", None, None),
            P("req", "head"),
            P(None, "head"),
            P(None, "head", None, None),
            P("head"),
            P("head"),
            P("head"),
            P("head"),
            P("req"),
            P(),
            P("req"),
            P("req"),
            P("req", "head", None),
            P("req", None, "head"),
            P("req", "head", None, None),
            P("req", None, "head"),
            P("req", None, "head", None, None),
        ),
        out_specs=(P("req", "head"), P("req", "head"), P("req", "head", None, None)),
        check_vma=False,
    )
```

profile of v0, /device:TPU:16, one launch (start us, length us, event | category | flops | bytes accessed | tf_op | source)
XLA Modules:
  0.0 330.3 jit_solution(10483867477987839845)
XLA Ops:
  0.6 0.8 all_to_all.109
  1.4 0.6 copy.93
  2.1 18.6 %all-to-all-start.2 = ((bf16[2,64,12]{2,0,1:T(2,128)(2,1)}), bf16[2,64,12]{2,0,1:T(2,128)(2,1)S(1)}, u32[]{:S(2)}, u32[]{:S(2)}) async-start(bf16[2,64,12]{2,0,1:T(2,128)(2,1)} %copy.93), calls=%async_computation.2 | async-start | bytes 65536 | tf_op jit(solution)/shard_map/all_to_all | solution.py:84
  22.6 1.3 dynamic-slice
  23.9 0.8 dynamic-update-slice
  24.7 0.8 dynamic-update-slice.1
  25.4 0.8 dynamic-update-slice.2
  26.2 25.0 %all-reduce.3 = (s32[64]{0:T(128)S(1)}, s32[64]{0:T(128)S(1)}, s32[64]{0:T(128)S(1)}) all-reduce(s32[64]{0:T(128)S(1)} %dynamic-update-slice.1, s32[64]{0:T(128)S(1)} %dynamic-update-slice, s32[64]{0:T(128)S(1)} %dynamic-update-slice.2), channel_id=1, replica_groups=mesh['req'=64,'head'=8] {'req'}, use_global_device_ids=true, to_apply=%add.1 | all-reduce | flops 192 | bytes 1536
  51.2 0.8 select_reduce_fusion
  52.1 0.8 copy.87
  52.9 0.7 copy.88
  53.6 1.1 copy.134
  55.3 1.4 reduce.10
  56.7 0.7 reshape.580
  57.5 13.3 %all-to-all-start = ((bf16[2,64,96]{2,0,1:T(2,128)(2,1)}), bf16[2,64,96]{2,0,1:T(2,128)(2,1)S(1)}, u32[]{:S(2)}, u32[]{:S(2)}) async-start(bf16[2,64,96]{2,0,1:T(2,128)(2,1)} %copy.88), calls=%async_computation | async-start | bytes 65536 | tf_op jit(solution)/shard_map/all_to_all | solution.py:83
  70.8 12.8 %all-to-all-done = bf16[2,64,96]{2,0,1:T(2,128)(2,1)S(1)} async-done(((bf16[2,64,96]{2,0,1:T(2,128)(2,1)}), bf16[2,64,96]{2,0,1:T(2,128)(2,1)S(1)}, u32[]{:S(2)}, u32[]{:S(2)}) %all-to-all-start) | async-done | bytes 24608 | tf_op jit(solution)/shard_map/all_to_all | solution.py:83
  83.6 6.2 %all-to-all-start.8 = ((bf16[64,2,512]{2,1,0:T(2,128)(2,1)}), bf16[64,2,512]{2,1,0:T(2,128)(2,1)S(1)}, u32[]{:S(2)}, u32[]{:S(2)}) async-start(bf16[64,2,512]{2,1,0:T(2,128)(2,1)} %reshape.580), calls=%async_computation.8 | async-start | bytes 262144 | tf_op jit(solution)/shard_map/all_to_all | solution.py:75
  89.9 0.6 gather_fusion.1
  90.6 0.6 copy.94
  91.2 0.6 gather_fusion
  91.9 12.9 %all-to-all-done.8 = bf16[64,2,512]{2,1,0:T(2,128)(2,1)S(1)} async-done(((bf16[64,2,512]{2,1,0:T(2,128)(2,1)}), bf16[64,2,512]{2,1,0:T(2,128)(2,1)S(1)}, u32[]{:S(2)}, u32[]{:S(2)}) %all-to-all-start.8) | async-done | bytes 131104 | tf_op jit(solution)/shard_map/all_to_all | solution.py:75
  104.8 5.9 %all-to-all-start.3 = ((bf16[64,1,12]{2,1,0:T(2,128)(2,1)}), bf16[64,1,12]{2,1,0:T(2,128)(2,1)S(1)}, u32[]{:S(2)}, u32[]{:S(2)}) async-start(bf16[64,1,12]{2,1,0:T(2,128)(2,1)} %copy.94), calls=%async_computation.3 | async-start | bytes 65536 | tf_op jit(solution)/shard_map/all_to_all | solution.py:96
  110.8 0.6 copy.89
  111.6 0.7 gather_fusion.4
  112.3 11.3 %all-to-all-done.3 = bf16[64,1,12]{2,1,0:T(2,128)(2,1)S(1)} async-done(((bf16[64,1,12]{2,1,0:T(2,128)(2,1)}), bf16[64,1,12]{2,1,0:T(2,128)(2,1)S(1)}, u32[]{:S(2)}, u32[]{:S(2)}) %all-to-all-start.3) | async-done | bytes 1568 | tf_op jit(solution)/shard_map/all_to_all | solution.py:96
  123.6 6.3 %all-to-all-start.1 = ((bf16[64,1,96]{2,1,0:T(2,128)(2,1)}), bf16[64,1,96]{2,1,0:T(2,128)(2,1)S(1)}, u32[]{:S(2)}, u32[]{:S(2)}) async-start(bf16[64,1,96]{2,1,0:T(2,128)(2,1)} %copy.89), calls=%async_computation.1 | async-start | bytes 65536 | tf_op jit(solution)/shard_map/all_to_all | solution.py:95
  130.1 0.7 reduce.11
  130.8 0.7 reshape.582
  131.5 11.3 %all-to-all-done.1 = bf16[64,1,96]{2,1,0:T(2,128)(2,1)S(1)} async-done(((bf16[64,1,96]{2,1,0:T(2,128)(2,1)}), bf16[64,1,96]{2,1,0:T(2,128)(2,1)S(1)}, u32[]{:S(2)}, u32[]{:S(2)}) %all-to-all-start.1) | async-done | bytes 12320 | tf_op jit(solution)/shard_map/all_to_all | solution.py:95
  142.9 6.4 %all-to-all-start.9 = ((bf16[64,2,512]{2,1,0:T(2,128)(2,1)}), bf16[64,2,512]{2,1,0:T(2,128)(2,1)S(1)}, u32[]{:S(2)}, u32[]{:S(2)}) async-start(bf16[64,2,512]{2,1,0:T(2,128)(2,1)} %reshape.582), calls=%async_computation.9 | async-start | bytes 262144 | tf_op jit(solution)/shard_map/all_to_all | solution.py:93
  149.9 2.2 reduce.12
  152.1 0.9 reshape.584
  153.0 10.8 %all-to-all-done.9 = bf16[64,2,512]{2,1,0:T(2,128)(2,1)S(1)} async-done(((bf16[64,2,512]{2,1,0:T(2,128)(2,1)}), bf16[64,2,512]{2,1,0:T(2,128)(2,1)S(1)}, u32[]{:S(2)}, u32[]{:S(2)}) %all-to-all-start.9) | async-done | bytes 131104 | tf_op jit(solution)/shard_map/all_to_all | solution.py:93
  163.8 0.6 copy-done.4
  164.4 6.6 %all-to-all-start.6 = ((bf16[64,2,1024]{2,1,0:T(2,128)(2,1)}), bf16[64,2,1024]{2,1,0:T(2,128)(2,1)S(1)}, u32[]{:S(2)}, u32[]{:S(2)}) async-start(bf16[64,2,1024]{2,1,0:T(2,128)(2,1)} %reshape.584), calls=%async_computation.6 | async-start | bytes 524288 | tf_op jit(solution)/shard_map/all_to_all | solution.py:68
  171.6 2.1 copy.100
  173.7 14.8 %all-to-all-done.6 = bf16[64,2,1024]{2,1,0:T(2,128)(2,1)S(1)} async-done(((bf16[64,2,1024]{2,1,0:T(2,128)(2,1)}), bf16[64,2,1024]{2,1,0:T(2,128)(2,1)S(1)}, u32[]{:S(2)}, u32[]{:S(2)}) %all-to-all-start.6) | async-done | bytes 262176 | tf_op jit(solution)/shard_map/all_to_all | solution.py:68
  188.4 6.1 %all-to-all-start.4 = ((bf16[2,64,4096]{2,0,1:T(2,128)(2,1)}), bf16[2,64,4096]{2,0,1:T(2,128)(2,1)S(1)}, u32[]{:S(2)}, u32[]{:S(2)}) async-start(bf16[2,64,4096]{2,0,1:T(2,128)(2,1)} %copy.100), calls=%async_computation.4 | async-start | bytes 2097152 | tf_op jit(solution)/shard_map/all_to_all | solution.py:82
  194.6 0.7 fusion.33
  196.3 0.7 gather_fusion.3
  197.1 0.8 reduce.13
  198.0 0.9 reshape.586
  198.8 38.3 %all-to-all-done.4 = bf16[2,64,4096]{2,0,1:T(2,128)(2,1)S(1)} async-done(((bf16[2,64,4096]{2,0,1:T(2,128)(2,1)}), bf16[2,64,4096]{2,0,1:T(2,128)(2,1)S(1)}, u32[]{:S(2)}, u32[]{:S(2)}) %all-to-all-start.4) | async-done | bytes 1048608 | tf_op jit(solution)/shard_map/all_to_all | solution.py:82
  237.1 5.9 %all-to-all-start.7 = ((bf16[64,2,1024]{2,1,0:T(2,128)(2,1)}), bf16[64,2,1024]{2,1,0:T(2,128)(2,1)S(1)}, u32[]{:S(2)}, u32[]{:S(2)}) async-start(bf16[64,2,1024]{2,1,0:T(2,128)(2,1)} %reshape.586), calls=%async_computation.7 | async-start | bytes 524288 | tf_op jit(solution)/shard_map/all_to_all | solution.py:92
  243.7 0.9 gather_fusion.2
  244.7 1.1 reduce.9
  245.9 1.2 reshape.578
  247.0 13.4 %all-to-all-done.7 = bf16[64,2,1024]{2,1,0:T(2,128)(2,1)S(1)} async-done(((bf16[64,2,1024]{2,1,0:T(2,128)(2,1)}), bf16[64,2,1024]{2,1,0:T(2,128)(2,1)S(1)}, u32[]{:S(2)}, u32[]{:S(2)}) %all-to-all-start.7) | async-done | bytes 262176 | tf_op jit(solution)/shard_map/all_to_all | solution.py:92
  260.4 5.8 %all-to-all-start.5 = ((bf16[64,2,2048]{2,1,0:T(2,128)(2,1)}), bf16[64,2,2048]{2,1,0:T(2,128)(2,1)S(1)}, u32[]{:S(2)}, u32[]{:S(2)}) async-start(bf16[64,2,2048]{2,1,0:T(2,128)(2,1)} %reshape.578), calls=%async_computation.5 | async-start | bytes 1048576 | tf_op jit(solution)/shard_map/all_to_all | solution.py:94
  266.6 0.6 copy.133
  267.3 0.6 copy.132
  269.7 0.7 iota_compare_fusion
  270.8 0.9 fusion.22
  272.2 3.8 %fusion.9 = (bf16[1,256,2048]{1,2,0:T(8,128)(2,1)}, bf16[1,256,2048]{1,2,0:T(8,128)(2,1)}) fusion(f32[256,32]{0,1:T(8,128)S(1)} %bitcast.165, bf16[256,2048]{0,1:T(8,128)(2,1)S(1)} %copy.90, f32[2048]{0:T(1024)S(1)} %bitcast.169, bf16[1,256,2048]{1,2,0:T(8,128)(2,1)S(1)} %bitcast.147, bf16[1,3,2048]{1,2,0:T(8,128)(2,1)S(1)} %copy.91, f32[2048]{0:T(1024)S(1)} %bitcast.170, ...), kind=kLoop, calls=%fused_computation.17 | loop fusion | flops 14680064 | bytes 4272128 | tf_op jit(solution)/shard_map/convert_element_type | solution.py:162
  276.4 1.5 reduce.5
  278.4 11.4 %all-to-all-done.5 = bf16[64,2,2048]{2,1,0:T(2,128)(2,1)S(1)} async-done(((bf16[64,2,2048]{2,1,0:T(2,128)(2,1)}), bf16[64,2,2048]{2,1,0:T(2,128)(2,1)S(1)}, u32[]{:S(2)}, u32[]{:S(2)}) %all-to-all-start.5) | async-done | bytes 524320 | tf_op jit(solution)/shard_map/all_to_all | solution.py:94
  290.3 3.1 reduce.4
  294.8 2.6 multiply_reduce_fusion
  297.8 1.0 convolution_bitcast_fusion
  298.8 24.5 %psum.7 = bf16[1,256,64]{1,2,0:T(8,128)(2,1)S(1)} all-reduce(f32[1,256,64]{1,2,0:T(8,128)} %convolution_bitcast_fusion), channel_id=1, replica_groups=mesh['req'=64,'head'=8] {'head'}, use_global_device_ids=true, to_apply=%region_4.5 | all-reduce | flops 16384 | bytes 98304 | tf_op jit(solution)/shard_map/psum | solution.py:153
  323.3 1.9 copy.102
  325.2 2.8 multiply_convert_fusion.3
  328.0 1.2 fusion.12
  329.2 1.1 fusion.10
  (102 shorter events, 10.1 us)
Async XLA Ops:
  2.1 55.4 %all-to-all-start.2 = ((bf16[2,64,12]{2,0,1:T(2,128)(2,1)}), bf16[2,64,12]{2,0,1:T(2,128)(2,1)S(1)}, u32[]{:S(2)}, u32[]{:S(2)}) async-start(bf16[2,64,12]{2,0,1:T(2,128)(2,1)} %copy.93), calls=%async_computation.2 | async-start | bytes 65536 | tf_op jit(solution)/shard_map/all_to_all | solution.py:84
  56.7 92.5 %copy-start.6 = (bf16[1,2048,64]{1,2,0:T(8,128)(2,1)S(1)}, bf16[1,2048,64]{1,2,0:T(8,128)(2,1)}, u32[]{:S(2)}) copy-start(bf16[1,2048,64]{1,2,0:T(8,128)(2,1)} %param.31) | copy-start | bytes 786436
  57.5 26.1 %all-to-all-start = ((bf16[2,64,96]{2,0,1:T(2,128)(2,1)}), bf16[2,64,96]{2,0,1:T(2,128)(2,1)S(1)}, u32[]{:S(2)}, u32[]{:S(2)}) async-start(bf16[2,64,96]{2,0,1:T(2,128)(2,1)} %copy.88), calls=%async_computation | async-start | bytes 65536 | tf_op jit(solution)/shard_map/all_to_all | solution.py:83
  83.6 21.2 %all-to-all-start.8 = ((bf16[64,2,512]{2,1,0:T(2,128)(2,1)}), bf16[64,2,512]{2,1,0:T(2,128)(2,1)S(1)}, u32[]{:S(2)}, u32[]{:S(2)}) async-start(bf16[64,2,512]{2,1,0:T(2,128)(2,1)} %reshape.580), calls=%async_computation.8 | async-start | bytes 262144 | tf_op jit(solution)/shard_map/all_to_all | solution.py:75
  104.8 18.8 %all-to-all-start.3 = ((bf16[64,1,12]{2,1,0:T(2,128)(2,1)}), bf16[64,1,12]{2,1,0:T(2,128)(2,1)S(1)}, u32[]{:S(2)}, u32[]{:S(2)}) async-start(bf16[64,1,12]{2,1,0:T(2,128)(2,1)} %copy.94), calls=%async_computation.3 | async-start | bytes 65536 | tf_op jit(solution)/shard_map/all_to_all | solution.py:96
  123.6 19.2 %all-to-all-start.1 = ((bf16[64,1,96]{2,1,0:T(2,128)(2,1)}), bf16[64,1,96]{2,1,0:T(2,128)(2,1)S(1)}, u32[]{:S(2)}, u32[]{:S(2)}) async-start(bf16[64,1,96]{2,1,0:T(2,128)(2,1)} %copy.89), calls=%async_computation.1 | async-start | bytes 65536 | tf_op jit(solution)/shard_map/all_to_all | solution.py:95
  130.8 40.3 %copy-start.1 = (bf16[2,32,64,128]{3,2,1,0:T(8,128)(2,1)S(1)}, bf16[2,32,64,128]{3,2,1,0:T(8,128)(2,1)}, u32[]{:S(2)}) copy-start(bf16[2,32,64,128]{3,2,1,0:T(8,128)(2,1)} %param.33) | copy-start | bytes 3145732
  142.9 20.9 %all-to-all-start.9 = ((bf16[64,2,512]{2,1,0:T(2,128)(2,1)}), bf16[64,2,512]{2,1,0:T(2,128)(2,1)S(1)}, u32[]{:S(2)}, u32[]{:S(2)}) async-start(bf16[64,2,512]{2,1,0:T(2,128)(2,1)} %reshape.582), calls=%async_computation.9 | async-start | bytes 262144 | tf_op jit(solution)/shard_map/all_to_all | solution.py:93
  163.8 0.7 copy-start.4
  164.4 24.0 %all-to-all-start.6 = ((bf16[64,2,1024]{2,1,0:T(2,128)(2,1)}), bf16[64,2,1024]{2,1,0:T(2,128)(2,1)S(1)}, u32[]{:S(2)}, u32[]{:S(2)}) async-start(bf16[64,2,1024]{2,1,0:T(2,128)(2,1)} %reshape.584), calls=%async_computation.6 | async-start | bytes 524288 | tf_op jit(solution)/shard_map/all_to_all | solution.py:68
  171.6 23.0 %copy-start.20 = (f32[32]{0:T(128)S(1)}, f32[32]{0:T(128)}, u32[]{:S(2)}) copy-start(f32[32]{0:T(128)} %param.24) | copy-start | bytes 388
  171.6 23.0 %copy-start.16 = (bf16[256,32]{0,1:T(8,128)(2,1)S(1)}, bf16[256,32]{0,1:T(8,128)(2,1)}, u32[]{:S(2)}) copy-start(bf16[256,32]{0,1:T(8,128)(2,1)} %param.20) | copy-start | bytes 49156
  171.6 23.0 %copy-start.18 = (f32[32]{0:T(128)S(1)}, f32[32]{0:T(128)}, u32[]{:S(2)}) copy-start(f32[32]{0:T(128)} %param.23) | copy-start | bytes 388
  188.4 48.7 %all-to-all-start.4 = ((bf16[2,64,4096]{2,0,1:T(2,128)(2,1)}), bf16[2,64,4096]{2,0,1:T(2,128)(2,1)S(1)}, u32[]{:S(2)}, u32[]{:S(2)}) async-start(bf16[2,64,4096]{2,0,1:T(2,128)(2,1)} %copy.100), calls=%async_computation.4 | async-start | bytes 2097152 | tf_op jit(solution)/shard_map/all_to_all | solution.py:82
  237.1 23.3 %all-to-all-start.7 = ((bf16[64,2,1024]{2,1,0:T(2,128)(2,1)}), bf16[64,2,1024]{2,1,0:T(2,128)(2,1)S(1)}, u32[]{:S(2)}, u32[]{:S(2)}) async-start(bf16[64,2,1024]{2,1,0:T(2,128)(2,1)} %reshape.586), calls=%async_computation.7 | async-start | bytes 524288 | tf_op jit(solution)/shard_map/all_to_all | solution.py:92
  244.6 21.8 %copy-start.10 = (f32[2048]{0:T(1024)S(1)}, f32[2048]{0:T(1024)}, u32[]{:S(2)}) copy-start(f32[2048]{0:T(1024)} %param.26) | copy-start | bytes 24580
  244.7 24.4 %copy-start.8 = (bf16[256,1,2,128]{3,2,1,0:T(2,128)(2,1)S(1)}, bf16[256,1,2,128]{3,2,1,0:T(2,128)(2,1)}, u32[]{:S(2)}) copy-start(bf16[256,1,2,128]{3,2,1,0:T(2,128)(2,1)} %param.19) | copy-start | bytes 393220
  244.7 24.4 %copy-start.2 = (bf16[256,2048]{1,0:T(8,128)(2,1)S(1)}, bf16[256,2048]{1,0:T(8,128)(2,1)}, u32[]{:S(2)}) copy-start(bf16[256,2048]{1,0:T(8,128)(2,1)} %param.18) | copy-start | bytes 3145732
  247.0 23.3 %copy-start.17 = (f32[4,1,2,128]{3,2,1,0:T(2,128)S(1)}, f32[4,1,2,128]{3,2,1,0:T(2,128)}, u32[]{:S(2)}) copy-start(f32[4,1,2,128]{3,2,1,0:T(2,128)} %param.22) | copy-start | bytes 12292
  247.0 23.3 %copy-start.13 = (f32[4,2048]{1,0:T(4,128)S(1)}, f32[4,2048]{1,0:T(4,128)}, u32[]{:S(2)}) copy-start(f32[4,2048]{1,0:T(4,128)} %param.21) | copy-start | bytes 98308
  260.4 29.4 %all-to-all-start.5 = ((bf16[64,2,2048]{2,1,0:T(2,128)(2,1)}), bf16[64,2,2048]{2,1,0:T(2,128)(2,1)S(1)}, u32[]{:S(2)}, u32[]{:S(2)}) async-start(bf16[64,2,2048]{2,1,0:T(2,128)(2,1)} %reshape.578), calls=%async_computation.5 | async-start | bytes 1048576 | tf_op jit(solution)/shard_map/all_to_all | solution.py:94
  272.2 3.8 %copy-start.5 = (bf16[64,2,512]{2,1,0:T(2,128)(2,1)S(1)}, bf16[64,2,512]{2,1,0:T(2,128)(2,1)}, u32[]{:S(2)}) copy-start(bf16[64,2,512]{2,1,0:T(2,128)(2,1)} %copy-done.4) | copy-start | bytes 393220
  293.5 1.2 copy-start.3
  293.5 1.3 copy-start.7
  293.5 1.2 copy-start.9
  293.5 1.2 copy-start.12
  293.5 1.2 copy-start.14
  293.5 1.2 copy-start.15
  293.6 1.2 copy-start.21
  323.3 1.9 copy-start.11
  325.2 2.8 copy-start
  325.2 2.8 copy-start.19
where the time goes:
time: 331 us; the launch traced here: 330 us
  waiting for transfers between devices  137 us (41%)
  starting transfers between devices  81.3 us (25%)
  blocking collectives  49.5 us (15%)
  local copies, waits for them, and re-layouts  30.2 us (9%)
  other arithmetic  21.9 us (7%)
  matrix products  7.25 us (2%)
    all_to_all x1, waiting for transfers between devices, per_device(): lax.all_to_all(ssm_flat, 'req', split_axis=1, concat_axis=0, tiled=True)  38.3 us
    unnamed x1, blocking collectives  25 us
    psum x1, blocking collectives, per_device(): reduced_rank = lax.psum(low_partial, 'head').astype(jnp.bfloat16)  24.5 us
    all_to_all x1, starting transfers between devices, per_device(): lax.all_to_all(convbc_flat, 'req', split_axis=1, concat_axis=0, tiled=True)  18.6 us
    all_to_all x1, waiting for transfers between devices, per_device(): lax.all_to_all(adapter_down_panels.reshape(adapter_down_panels.shape[0],...  14.8 us
    unnamed x71, local copies, waits for them, and re-layouts  14.5 us
    all_to_all x1, waiting for transfers between devices, per_device(): lax.all_to_all(picked_left_factor, 'req', split_axis=0, concat_axis=1, ti...  13.4 us
    all_to_all x1, starting transfers between devices, per_device(): lax.all_to_all(convx_flat, 'req', split_axis=1, concat_axis=0, tiled=True)  13.3 us
  transfers between devices with their start and end apart: 10, of which 9 were waited for; matrix products, arithmetic and copies ran while one was open for 12% of the time, Pallas kernels for 0%

commit v1 on v0

--- a/solution.py
+++ b/solution.py
@@ -92,7 +92,12 @@
         lax.all_to_all(picked_left_factor, "req", split_axis=0, concat_axis=1, tiled=True),
         lax.all_to_all(picked_right_factor, "req", split_axis=0, concat_axis=1, tiled=True),
         lax.all_to_all(chosen_state, "req", split_axis=0, concat_axis=1, tiled=True),
-        lax.all_to_all(chosen_convx, "req", split_axis=0, concat_axis=1, tiled=True),
+        jnp.concatenate(
+            lax.all_to_all(
+                jnp.stack(jnp.split(chosen_convx, lax.axis_size("req"), axis=0)), "req", 0, 0
+            ),
+            axis=1,
+        ),
         lax.all_to_all(chosen_convbc, "req", split_axis=0, concat_axis=1, tiled=True),
     )
     down_panel = fetched[0].reshape(per_device_share, hidden_features_on_card, reduced_width)

time: 331 us -> 360 us (1.088)
  the two profiles are of different devices: /device:TPU:16 before, /device:TPU:8 now
where the time goes in v1:
time: 360 us; the launch traced here: 359 us
  waiting for transfers between devices  128 us (36%)
  starting transfers between devices  84.8 us (24%)
  local copies, waits for them, and re-layouts  62.4 us (17%)
  blocking collectives  51 us (14%)
  other arithmetic  21.9 us (6%)
  matrix products  7.24 us (2%)
    unnamed x134, local copies, waits for them, and re-layouts  46.9 us
    all_to_all x1, waiting for transfers between devices, per_device(): lax.all_to_all(ssm_flat, 'req', split_axis=1, concat_axis=0, tiled=True)  38.8 us
    unnamed x1, blocking collectives  26.5 us
    psum x1, blocking collectives, per_device(): reduced_rank = lax.psum(low_partial, 'head').astype(jnp.bfloat16)  24.5 us
    all_to_all x1, starting transfers between devices, per_device(): lax.all_to_all(convbc_flat, 'req', split_axis=1, concat_axis=0, tiled=True)  18.7 us
    all_to_all x1, waiting for transfers between devices, per_device(): lax.all_to_all(adapter_down_panels.reshape(adapter_down_panels.shape[0],...  15.3 us
    all_to_all x1, starting transfers between devices, per_device(): lax.all_to_all(chosen_convbc, 'req', split_axis=0, concat_axis=1, tiled=T...  15.2 us
    all_to_all x1, waiting for transfers between devices, per_device(): lax.all_to_all(picked_left_factor, 'req', split_axis=0, concat_axis=1, ti...  13.9 us
  transfers between devices with their start and end apart: 10, of which 8 were waited for; matrix products, arithmetic and copies ran while one was open for 20% of the time, Pallas kernels for 0%

profile of v1, /device:TPU:8, one launch (start us, length us, event | category | flops | bytes accessed | tf_op | source)
XLA Modules:
  0.0 358.5 jit_solution(16805403306066026485)
XLA Ops:
  0.6 0.8 all_to_all.104
  1.4 0.6 copy.91
  2.1 18.7 %all-to-all-start.2 = ((bf16[2,64,12]{2,0,1:T(2,128)(2,1)}), bf16[2,64,12]{2,0,1:T(2,128)(2,1)S(1)}, u32[]{:S(2)}, u32[]{:S(2)}) async-start(bf16[2,64,12]{2,0,1:T(2,128)(2,1)} %copy.91), calls=%async_computation.2 | async-start | bytes 65536 | tf_op jit(solution)/shard_map/all_to_all | solution.py:84
  22.8 1.3 dynamic-slice
  24.0 0.8 dynamic-update-slice
  24.8 0.8 dynamic-update-slice.1
  25.5 0.8 dynamic-update-slice.2
  26.3 26.5 %all-reduce.3 = (s32[64]{0:T(128)S(1)}, s32[64]{0:T(128)S(1)}, s32[64]{0:T(128)S(1)}) all-reduce(s32[64]{0:T(128)S(1)} %dynamic-update-slice.1, s32[64]{0:T(128)S(1)} %dynamic-update-slice, s32[64]{0:T(128)S(1)} %dynamic-update-slice.2), channel_id=1, replica_groups=mesh['req'=64,'head'=8] {'req'}, use_global_device_ids=true, to_apply=%add.1 | all-reduce | flops 192 | bytes 1536
  52.9 0.8 select_reduce_fusion
  53.8 0.8 copy.86
  54.6 0.7 copy.87
  55.3 1.1 copy.132
  56.4 0.6 broadcast.248
  57.0 1.4 reduce.10
  58.4 0.7 reshape.545
  59.1 11.8 %all-to-all-start = ((bf16[2,64,96]{2,0,1:T(2,128)(2,1)}), bf16[2,64,96]{2,0,1:T(2,128)(2,1)S(1)}, u32[]{:S(2)}, u32[]{:S(2)}) async-start(bf16[2,64,96]{2,0,1:T(2,128)(2,1)} %copy.87), calls=%async_computation | async-start | bytes 65536 | tf_op jit(solution)/shard_map/all_to_all | solution.py:83
  70.9 0.6 gather_fusion.1
  71.7 0.6 copy.92
  72.3 12.2 %all-to-all-done = bf16[2,64,96]{2,0,1:T(2,128)(2,1)S(1)} async-done(((bf16[2,64,96]{2,0,1:T(2,128)(2,1)}), bf16[2,64,96]{2,0,1:T(2,128)(2,1)S(1)}, u32[]{:S(2)}, u32[]{:S(2)}) %all-to-all-start) | async-done | bytes 24608 | tf_op jit(solution)/shard_map/all_to_all | solution.py:83
  84.5 5.5 %all-to-all-start.8 = ((bf16[64,2,512]{2,1,0:T(2,128)(2,1)}), bf16[64,2,512]{2,1,0:T(2,128)(2,1)S(1)}, u32[]{:S(2)}, u32[]{:S(2)}) async-start(bf16[64,2,512]{2,1,0:T(2,128)(2,1)} %reshape.545), calls=%async_computation.8 | async-start | bytes 262144 | tf_op jit(solution)/shard_map/all_to_all | solution.py:75
  90.0 0.6 gather_fusion
  123.1 15.2 %all-to-all-start.3 = ((bf16[64,1,12]{2,1,0:T(2,128)(2,1)}), bf16[64,1,12]{2,1,0:T(2,128)(2,1)S(1)}, u32[]{:S(2)}, u32[]{:S(2)}) async-start(bf16[64,1,12]{2,1,0:T(2,128)(2,1)} %copy.92), calls=%async_computation.3 | async-start | bytes 65536 | tf_op jit(solution)/shard_map/all_to_all | solution.py:101
  139.0 0.7 gather_fusion.4
  139.7 12.3 %all-to-all-done.3 = bf16[64,1,12]{2,1,0:T(2,128)(2,1)S(1)} async-done(((bf16[64,1,12]{2,1,0:T(2,128)(2,1)}), bf16[64,1,12]{2,1,0:T(2,128)(2,1)S(1)}, u32[]{:S(2)}, u32[]{:S(2)}) %all-to-all-start.3) | async-done | bytes 1568 | tf_op jit(solution)/shard_map/all_to_all | solution.py:101
  152.1 5.3 %all-to-all-start.1 = ((bf16[64,1,96]{2,1,0:T(2,128)(2,1)}), bf16[64,1,96]{2,1,0:T(2,128)(2,1)S(1)}, u32[]{:S(2)}, u32[]{:S(2)}) async-start(bf16[64,1,96]{2,1,0:T(2,128)(2,1)} %constant_dynamic-update-slice_fusion), calls=%async_computation.1 | async-start | bytes 65536 | tf_op jit(solution)/shard_map/all_to_all | solution.py:96
  157.5 0.7 reduce.11
  158.2 0.7 reshape.547
  158.9 12.1 %all-to-all-done.1 = bf16[64,1,96]{2,1,0:T(2,128)(2,1)S(1)} async-done(((bf16[64,1,96]{2,1,0:T(2,128)(2,1)}), bf16[64,1,96]{2,1,0:T(2,128)(2,1)S(1)}, u32[]{:S(2)}, u32[]{:S(2)}) %all-to-all-start.1) | async-done | bytes 12320 | tf_op jit(solution)/shard_map/all_to_all | solution.py:96
  171.0 5.6 %all-to-all-start.9 = ((bf16[64,2,512]{2,1,0:T(2,128)(2,1)}), bf16[64,2,512]{2,1,0:T(2,128)(2,1)S(1)}, u32[]{:S(2)}, u32[]{:S(2)}) async-start(bf16[64,2,512]{2,1,0:T(2,128)(2,1)} %reshape.547), calls=%async_computation.9 | async-start | bytes 262144 | tf_op jit(solution)/shard_map/all_to_all | solution.py:93
  177.3 2.2 reduce.12
  179.5 0.9 reshape.549
  180.4 11.7 %all-to-all-done.9 = bf16[64,2,512]{2,1,0:T(2,128)(2,1)S(1)} async-done(((bf16[64,2,512]{2,1,0:T(2,128)(2,1)}), bf16[64,2,512]{2,1,0:T(2,128)(2,1)S(1)}, u32[]{:S(2)}, u32[]{:S(2)}) %all-to-all-start.9) | async-done | bytes 131104 | tf_op jit(solution)/shard_map/all_to_all | solution.py:93
  192.0 0.6 copy-done.4
  192.7 5.8 %all-to-all-start.6 = ((bf16[64,2,1024]{2,1,0:T(2,128)(2,1)}), bf16[64,2,1024]{2,1,0:T(2,128)(2,1)S(1)}, u32[]{:S(2)}, u32[]{:S(2)}) async-start(bf16[64,2,1024]{2,1,0:T(2,128)(2,1)} %reshape.549), calls=%async_computation.6 | async-start | bytes 524288 | tf_op jit(solution)/shard_map/all_to_all | solution.py:68
  199.0 2.1 copy.98
  201.1 15.3 %all-to-all-done.6 = bf16[64,2,1024]{2,1,0:T(2,128)(2,1)S(1)} async-done(((bf16[64,2,1024]{2,1,0:T(2,128)(2,1)}), bf16[64,2,1024]{2,1,0:T(2,128)(2,1)S(1)}, u32[]{:S(2)}, u32[]{:S(2)}) %all-to-all-start.6) | async-done | bytes 262176 | tf_op jit(solution)/shard_map/all_to_all | solution.py:68
  216.3 5.6 %all-to-all-start.4 = ((bf16[2,64,4096]{2,0,1:T(2,128)(2,1)}), bf16[2,64,4096]{2,0,1:T(2,128)(2,1)S(1)}, u32[]{:S(2)}, u32[]{:S(2)}) async-start(bf16[2,64,4096]{2,0,1:T(2,128)(2,1)} %copy.98), calls=%async_computation.4 | async-start | bytes 2097152 | tf_op jit(solution)/shard_map/all_to_all | solution.py:82
  222.0 0.7 fusion.33
  222.7 0.6 reduce-window.6
  223.7 0.7 gather_fusion.3
  224.5 0.8 reduce.13
  225.4 0.9 reshape.551
  226.2 38.8 %all-to-all-done.4 = bf16[2,64,4096]{2,0,1:T(2,128)(2,1)S(1)} async-done(((bf16[2,64,4096]{2,0,1:T(2,128)(2,1)}), bf16[2,64,4096]{2,0,1:T(2,128)(2,1)S(1)}, u32[]{:S(2)}, u32[]{:S(2)}) %all-to-all-start.4) | async-done | bytes 1048608 | tf_op jit(solution)/shard_map/all_to_all | solution.py:82
  265.0 5.9 %all-to-all-start.7 = ((bf16[64,2,1024]{2,1,0:T(2,128)(2,1)}), bf16[64,2,1024]{2,1,0:T(2,128)(2,1)S(1)}, u32[]{:S(2)}, u32[]{:S(2)}) async-start(bf16[64,2,1024]{2,1,0:T(2,128)(2,1)} %reshape.551), calls=%async_computation.7 | async-start | bytes 524288 | tf_op jit(solution)/shard_map/all_to_all | solution.py:92
  271.6 0.9 gather_fusion.2
  272.6 1.1 reduce.9
  273.7 1.2 reshape.543
  274.9 13.9 %all-to-all-done.7 = bf16[64,2,1024]{2,1,0:T(2,128)(2,1)S(1)} async-done(((bf16[64,2,1024]{2,1,0:T(2,128)(2,1)}), bf16[64,2,1024]{2,1,0:T(2,128)(2,1)S(1)}, u32[]{:S(2)}, u32[]{:S(2)}) %all-to-all-start.7) | async-done | bytes 262176 | tf_op jit(solution)/shard_map/all_to_all | solution.py:92
  288.8 5.4 %all-to-all-start.5 = ((bf16[64,2,2048]{2,1,0:T(2,128)(2,1)}), bf16[64,2,2048]{2,1,0:T(2,128)(2,1)S(1)}, u32[]{:S(2)}, u32[]{:S(2)}) async-start(bf16[64,2,2048]{2,1,0:T(2,128)(2,1)} %reshape.543), calls=%async_computation.5 | async-start | bytes 1048576 | tf_op jit(solution)/shard_map/all_to_all | solution.py:94
  294.5 0.6 copy.131
  295.2 0.6 copy.130
  297.6 0.7 iota_compare_fusion
  298.7 0.9 fusion.22
  300.1 3.8 %fusion.9 = (bf16[1,256,2048]{1,2,0:T(8,128)(2,1)}, bf16[1,256,2048]{1,2,0:T(8,128)(2,1)}) fusion(f32[256,32]{0,1:T(8,128)S(1)} %bitcast.419, bf16[256,2048]{0,1:T(8,128)(2,1)S(1)} %copy.88, f32[2048]{0:T(1024)S(1)} %bitcast.423, bf16[1,256,2048]{1,2,0:T(8,128)(2,1)S(1)} %bitcast.401, bf16[1,3,2048]{1,2,0:T(8,128)(2,1)S(1)} %copy.89, f32[2048]{0:T(1024)S(1)} %bitcast.424, ...), kind=kLoop, calls=%fused_computation.17 | loop fusion | flops 14680064 | bytes 4272128 | tf_op jit(solution)/shard_map/convert_element_type | solution.py:167
  304.3 1.5 reduce.5
  306.3 11.7 %all-to-all-done.5 = bf16[64,2,2048]{2,1,0:T(2,128)(2,1)S(1)} async-done(((bf16[64,2,2048]{2,1,0:T(2,128)(2,1)}), bf16[64,2,2048]{2,1,0:T(2,128)(2,1)S(1)}, u32[]{:S(2)}, u32[]{:S(2)}) %all-to-all-start.5) | async-done | bytes 524320 | tf_op jit(solution)/shard_map/all_to_all | solution.py:94
  318.5 3.1 reduce.4
  323.0 2.6 multiply_reduce_fusion
  326.0 1.0 convolution_bitcast_fusion
  327.0 24.5 %psum.7 = bf16[1,256,64]{1,2,0:T(8,128)(2,1)S(1)} all-reduce(f32[1,256,64]{1,2,0:T(8,128)} %convolution_bitcast_fusion), channel_id=1, replica_groups=mesh['req'=64,'head'=8] {'head'}, use_global_device_ids=true, to_apply=%region_4.5 | all-reduce | flops 16384 | bytes 98304 | tf_op jit(solution)/shard_map/psum | solution.py:158
  351.5 1.9 copy.100
  353.3 2.8 multiply_convert_fusion.3
  356.2 1.2 fusion.12
  357.4 1.1 fusion.10
  (165 shorter events, 41.9 us)
Async XLA Ops:
  2.1 57.1 %all-to-all-start.2 = ((bf16[2,64,12]{2,0,1:T(2,128)(2,1)}), bf16[2,64,12]{2,0,1:T(2,128)(2,1)S(1)}, u32[]{:S(2)}, u32[]{:S(2)}) async-start(bf16[2,64,12]{2,0,1:T(2,128)(2,1)} %copy.91), calls=%async_computation.2 | async-start | bytes 65536 | tf_op jit(solution)/shard_map/all_to_all | solution.py:84
  58.4 118.2 %copy-start.6 = (bf16[1,2048,64]{1,2,0:T(8,128)(2,1)S(1)}, bf16[1,2048,64]{1,2,0:T(8,128)(2,1)}, u32[]{:S(2)}) copy-start(bf16[1,2048,64]{1,2,0:T(8,128)(2,1)} %param.31) | copy-start | bytes 786436
  59.1 25.3 %all-to-all-start = ((bf16[2,64,96]{2,0,1:T(2,128)(2,1)}), bf16[2,64,96]{2,0,1:T(2,128)(2,1)S(1)}, u32[]{:S(2)}, u32[]{:S(2)}) async-start(bf16[2,64,96]{2,0,1:T(2,128)(2,1)} %copy.87), calls=%async_computation | async-start | bytes 65536 | tf_op jit(solution)/shard_map/all_to_all | solution.py:83
  84.5 38.7 %all-to-all-start.8 = ((bf16[64,2,512]{2,1,0:T(2,128)(2,1)}), bf16[64,2,512]{2,1,0:T(2,128)(2,1)S(1)}, u32[]{:S(2)}, u32[]{:S(2)}) async-start(bf16[64,2,512]{2,1,0:T(2,128)(2,1)} %reshape.545), calls=%async_computation.8 | async-start | bytes 262144 | tf_op jit(solution)/shard_map/all_to_all | solution.py:75
  123.1 28.9 %all-to-all-start.3 = ((bf16[64,1,12]{2,1,0:T(2,128)(2,1)}), bf16[64,1,12]{2,1,0:T(2,128)(2,1)S(1)}, u32[]{:S(2)}, u32[]{:S(2)}) async-start(bf16[64,1,12]{2,1,0:T(2,128)(2,1)} %copy.92), calls=%async_computation.3 | async-start | bytes 65536 | tf_op jit(solution)/shard_map/all_to_all | solution.py:101
  152.1 18.9 %all-to-all-start.1 = ((bf16[64,1,96]{2,1,0:T(2,128)(2,1)}), bf16[64,1,96]{2,1,0:T(2,128)(2,1)S(1)}, u32[]{:S(2)}, u32[]{:S(2)}) async-start(bf16[64,1,96]{2,1,0:T(2,128)(2,1)} %constant_dynamic-update-slice_fusion), calls=%async_computation.1 | async-start | bytes 65536 | tf_op jit(solution)/shard_map/all_to_all | solution.py:96
  158.2 40.3 %copy-start.1 = (bf16[2,32,64,128]{3,2,1,0:T(8,128)(2,1)S(1)}, bf16[2,32,64,128]{3,2,1,0:T(8,128)(2,1)}, u32[]{:S(2)}) copy-start(bf16[2,32,64,128]{3,2,1,0:T(8,128)(2,1)} %param.33) | copy-start | bytes 3145732
  171.0 21.0 %all-to-all-start.9 = ((bf16[64,2,512]{2,1,0:T(2,128)(2,1)}), bf16[64,2,512]{2,1,0:T(2,128)(2,1)S(1)}, u32[]{:S(2)}, u32[]{:S(2)}) async-start(bf16[64,2,512]{2,1,0:T(2,128)(2,1)} %reshape.547), calls=%async_computation.9 | async-start | bytes 262144 | tf_op jit(solution)/shard_map/all_to_all | solution.py:93
  192.0 0.7 copy-start.4
  192.7 23.7 %all-to-all-start.6 = ((bf16[64,2,1024]{2,1,0:T(2,128)(2,1)}), bf16[64,2,1024]{2,1,0:T(2,128)(2,1)S(1)}, u32[]{:S(2)}, u32[]{:S(2)}) async-start(bf16[64,2,1024]{2,1,0:T(2,128)(2,1)} %reshape.549), calls=%async_computation.6 | async-start | bytes 524288 | tf_op jit(solution)/shard_map/all_to_all | solution.py:68
  199.0 23.0 %copy-start.20 = (f32[32]{0:T(128)S(1)}, f32[32]{0:T(128)}, u32[]{:S(2)}) copy-start(f32[32]{0:T(128)} %param.24) | copy-start | bytes 388
  199.0 23.0 %copy-start.16 = (bf16[256,32]{0,1:T(8,128)(2,1)S(1)}, bf16[256,32]{0,1:T(8,128)(2,1)}, u32[]{:S(2)}) copy-start(bf16[256,32]{0,1:T(8,128)(2,1)} %param.20) | copy-start | bytes 49156
  199.0 23.0 %copy-start.18 = (f32[32]{0:T(128)S(1)}, f32[32]{0:T(128)}, u32[]{:S(2)}) copy-start(f32[32]{0:T(128)} %param.23) | copy-start | bytes 388
  216.3 48.7 %all-to-all-start.4 = ((bf16[2,64,4096]{2,0,1:T(2,128)(2,1)}), bf16[2,64,4096]{2,0,1:T(2,128)(2,1)S(1)}, u32[]{:S(2)}, u32[]{:S(2)}) async-start(bf16[2,64,4096]{2,0,1:T(2,128)(2,1)} %copy.98), calls=%async_computation.4 | async-start | bytes 2097152 | tf_op jit(solution)/shard_map/all_to_all | solution.py:82
  265.0 23.8 %all-to-all-start.7 = ((bf16[64,2,1024]{2,1,0:T(2,128)(2,1)}), bf16[64,2,1024]{2,1,0:T(2,128)(2,1)S(1)}, u32[]{:S(2)}, u32[]{:S(2)}) async-start(bf16[64,2,1024]{2,1,0:T(2,128)(2,1)} %reshape.551), calls=%async_computation.7 | async-start | bytes 524288 | tf_op jit(solution)/shard_map/all_to_all | solution.py:92
  272.4 21.8 %copy-start.10 = (f32[2048]{0:T(1024)S(1)}, f32[2048]{0:T(1024)}, u32[]{:S(2)}) copy-start(f32[2048]{0:T(1024)} %param.26) | copy-start | bytes 24580
  272.6 24.4 %copy-start.8 = (bf16[256,1,2,128]{3,2,1,0:T(2,128)(2,1)S(1)}, bf16[256,1,2,128]{3,2,1,0:T(2,128)(2,1)}, u32[]{:S(2)}) copy-start(bf16[256,1,2,128]{3,2,1,0:T(2,128)(2,1)} %param.19) | copy-start | bytes 393220
  272.6 24.4 %copy-start.2 = (bf16[256,2048]{1,0:T(8,128)(2,1)S(1)}, bf16[256,2048]{1,0:T(8,128)(2,1)}, u32[]{:S(2)}) copy-start(bf16[256,2048]{1,0:T(8,128)(2,1)} %param.18) | copy-start | bytes 3145732
  274.9 23.3 %copy-start.17 = (f32[4,1,2,128]{3,2,1,0:T(2,128)S(1)}, f32[4,1,2,128]{3,2,1,0:T(2,128)}, u32[]{:S(2)}) copy-start(f32[4,1,2,128]{3,2,1,0:T(2,128)} %param.22) | copy-start | bytes 12292
  274.9 23.3 %copy-start.13 = (f32[4,2048]{1,0:T(4,128)S(1)}, f32[4,2048]{1,0:T(4,128)}, u32[]{:S(2)}) copy-start(f32[4,2048]{1,0:T(4,128)} %param.21) | copy-start | bytes 98308
  288.8 29.2 %all-to-all-start.5 = ((bf16[64,2,2048]{2,1,0:T(2,128)(2,1)}), bf16[64,2,2048]{2,1,0:T(2,128)(2,1)S(1)}, u32[]{:S(2)}, u32[]{:S(2)}) async-start(bf16[64,2,2048]{2,1,0:T(2,128)(2,1)} %reshape.543), calls=%async_computation.5 | async-start | bytes 1048576 | tf_op jit(solution)/shard_map/all_to_all | solution.py:94
  300.1 3.8 %copy-start.5 = (bf16[64,2,512]{2,1,0:T(2,128)(2,1)S(1)}, bf16[64,2,512]{2,1,0:T(2,128)(2,1)}, u32[]{:S(2)}) copy-start(bf16[64,2,512]{2,1,0:T(2,128)(2,1)} %copy-done.4) | copy-start | bytes 393220
  321.7 1.2 copy-start.3
  321.7 1.3 copy-start.7
  321.7 1.2 copy-start.9
  321.7 1.2 copy-start.12
  321.7 1.2 copy-start.14
  321.7 1.2 copy-start.15
  321.7 1.2 copy-start.21
  351.5 1.9 copy-start.11
  353.3 2.8 copy-start
  353.3 2.8 copy-start.19
